TPU v7x, 32 devices: a whole 2x2x4 slice. The times are simulated.
32 devices in a mesh: island: 4 (over y, core), section: 4 (over z), tensor: 2 (over x).
Axes of the slice: x: 2, y: 2, z: 4, core: 2. Of those that a mesh axis runs over, the one named last changes fastest.
Arguments:
- hidden: bfloat16 [4, 4, 256, 8192], P('island', 'section', 'tensor'), may hold values from -6 to 6
- norm_gain: bfloat16 [4, 8192], P('section'), may hold values from 0.099609375 to 1.8984375
- grad_above: bfloat16 [4, 256, 8192], P('island', 'tensor'), may hold values from -6 to 6
- key_cot: bfloat16 [4, 4, 256, 1024], P('island', 'section', None, 'tensor'), may hold values from -6 to 6
- value_cot: bfloat16 [4, 4, 256, 1024], P('island', 'section', None, 'tensor'), may hold values from -6 to 6
- local_key: bfloat16 [4, 4, 8192, 1024], P('island', 'section', None, 'tensor'), may hold values from -6 to 6
- local_value: bfloat16 [4, 4, 8192, 1024], P('island', 'section', None, 'tensor'), may hold values from -6 to 6
- anchor_key: float32 [4, 8192, 1024], P('section', 'island', 'tensor'), may hold values from -6 to 6
- anchor_value: float32 [4, 8192, 1024], P('section', 'island', 'tensor'), may hold values from -6 to 6
- momentum_key: float32 [4, 8192, 1024], P('section', 'island', 'tensor'), may hold values from -4 to 4
- momentum_value: float32 [4, 8192, 1024], P('section', 'island', 'tensor'), may hold values from -4 to 4
Outputs:
- anchor_key_new: float32 [4, 8192, 1024], P('section', 'island', 'tensor')
- anchor_value_new: float32 [4, 8192, 1024], P('section', 'island', 'tensor')
- momentum_key_new: float32 [4, 8192, 1024], P('section', 'island', 'tensor')
- momentum_value_new: float32 [4, 8192, 1024], P('section', 'island', 'tensor')
- input_grad: bfloat16 [4, 4, 256, 8192], P('island', 'section', 'tensor')
All inputs are finite; a program needn't handle non-finite values.
Results may differ from a plain program's by a relative error of at most 0.024.
Values may be sent and summed in bfloat16 or wider, within the bound.
No kernel may reach another device: no remote copies, remote signals or barrier semaphores. Data moves between devices by JAX's collectives and lax.ppermute only.
A program may use at most 128 MiB of HBM per device.

v0:
```python
import jax
import jax.numpy as jnp
from jax import lax
from jax.sharding import PartitionSpec as P

epsilon = 1e-05
inner_rate = 0.5
outer_rate = 0.7
outer_beta = 0.9


def from_behind(block, axis, distance):
    devices = range(lax.axis_size(axis))
    route = [(i - distance, i) for i in devices if i - distance in devices]
    return lax.ppermute(block, axis, route)


def contract_rows(left, right):
    return lax.dot_general(
        left, right, (((0,), (0,)), ((), ())), preferred_element_type=jnp.float32
    )


def contract_cols(left, right):
    return lax.dot_general(
        left, right, (((1,), (1,)), ((), ())), preferred_element_type=jnp.float32
    )


def outer_update(anchor, momentum, mean_delta):
    momentum_new = outer_beta * momentum + mean_delta
    return (anchor - outer_rate * (mean_delta + outer_beta * momentum_new), momentum_new)


def local(
    hidden,
    norm_gain,
    grad_above,
    key_cot,
    value_cot,
    local_key,
    local_value,
    anchor_key,
    anchor_value,
    momentum_key,
    momentum_value,
):
    resid = hidden[0, 0].astype(jnp.float32)
    gains = norm_gain[0].astype(jnp.float32)
    features = resid.shape[1]
    factor = float(features) ** (-0.5)
    inverse_rms = lax.rsqrt(jnp.mean(resid * resid, axis=-1, keepdims=True) + epsilon)
    normed = (resid * inverse_rms * gains).astype(jnp.bfloat16)
    key_rows = key_cot[0, 0]
    value_rows = value_cot[0, 0]
    weight_key = local_key[0, 0]
    weight_value = local_value[0, 0]
    piece = lax.all_gather(normed, "tensor", axis=0, tiled=True)
    key_piece = key_rows
    value_piece = value_rows
    grad_key = contract_rows(piece, key_piece)
    grad_value = contract_rows(piece, value_piece)
    new_key = weight_key.astype(jnp.float32) - inner_rate * (grad_key * factor)
    new_value = weight_value.astype(jnp.float32) - inner_rate * (grad_value * factor)
    key_piece = key_rows
    value_piece = value_rows
    upstream = lax.psum_scatter(
        (
            (contract_cols(key_piece, weight_key) + contract_cols(value_piece, weight_value))
            * factor
        ).astype(jnp.bfloat16),
        "tensor",
        scatter_dimension=0,
        tiled=True,
    ).astype(jnp.float32)
    scaled = gains * upstream
    branch = inverse_rms * scaled - resid * inverse_rms**3 * jnp.mean(
        resid * scaled, axis=-1, keepdims=True
    )
    is_top = (lax.axis_index("section") == lax.axis_size("section") - 1).astype(jnp.float32)
    own_term = branch + is_top * grad_above[0].astype(jnp.float32)
    running = own_term
    for turn in range(lax.axis_size("section") - 1):
        running = own_term + from_behind(running.astype(jnp.bfloat16), "section", -1).astype(
            running.dtype
        )
    input_grad = running.astype(jnp.bfloat16)[None, None]
    islands = lax.axis_size("island")
    summed_key, summed_value = (
        lax.psum_scatter(
            new_key.astype(jnp.bfloat16), "island", scatter_dimension=0, tiled=True
        ).astype(jnp.float32),
        lax.psum_scatter(
            new_value.astype(jnp.bfloat16), "island", scatter_dimension=0, tiled=True
        ).astype(jnp.float32),
    )
    mean_key = anchor_key[0] - summed_key / islands
    mean_value = anchor_value[0] - summed_value / islands
    anchor_key_new, momentum_key_new = outer_update(anchor_key[0], momentum_key[0], mean_key)
    anchor_value_new, momentum_value_new = outer_update(
        anchor_value[0], momentum_value[0], mean_value
    )
    return (
        anchor_key_new[None],
        anchor_value_new[None],
        momentum_key_new[None],
        momentum_value_new[None],
        input_grad,
    )


def solution(mesh):
    placed = (
        P("island", "section", "tensor", None),
        P("section", None),
        P("island", "tensor", None),
        P("island", "section", None, "tensor"),
        P("island", "section", None, "tensor"),
        P("island", "section", None, "tensor"),
        P("island", "section", None, "tensor"),
        P("section", "island", "tensor"),
        P("section", "island", "tensor"),
        P("section", "island", "tensor"),
        P("section", "island", "tensor"),
    )
    return jax.shard_map(
        local,
        mesh=mesh,
        in_specs=placed,
        out_specs=(
            P("section", "island", "tensor"),
            P("section", "island", "tensor"),
            P("section", "island", "tensor"),
            P("section", "island", "tensor"),
            P("island", "section", "tensor", None),
        ),
        check_vma=False,
    )
```

profile of v0, /device:TPU:0, one launch (start us, length us, event | category | flops | bytes accessed | tf_op | source)
XLA Modules:
  0.0 336.5 jit_solution(11189967100800048256)
XLA Ops:
  7.2 0.9 copy-done
  8.1 5.8 %fusion.3 = f32[256,8192]{1,0:T(8,128)S(1)} fusion(bf16[1,1,8192,512]{3,2,1,0:T(8,128)(2,1)} %param.16, bf16[1,1,256,512]{3,2,1,0:T(8,128)(2,1)S(1)} %copy-done), kind=kOutput, calls=%fused_computation.6 | convolution fusion | flops 2147483648 | bytes 17039360 | tf_op jit(solution)/shard_map/dot_general | solution.py:25
  13.9 7.9 %fusion.1 = bf16[256,8192]{1,0:T(8,128)(2,1)} fusion(f32[256,8192]{1,0:T(8,128)S(1)} %fusion.3, bf16[1,1,8192,512]{3,2,1,0:T(8,128)(2,1)} %param.17, bf16[1,1,256,512]{3,2,1,0:T(8,128)(2,1)S(1)} %copy-done.7), kind=kOutput, calls=%fused_computation.4 | convolution fusion | flops 2153775104 | bytes 21233664 | tf_op jit(solution)/shard_map/dot_general | solution.py:25
  21.8 0.0 all-gather.2.cloned.1.call-start
  21.9 0.7 copy-done.8
  22.6 56.5 %reduce-scatter.8.cloned.1.call-done = bf16[128,8192]{1,0:T(8,128)(2,1)} async-done(((bf16[256,8192]{1,0:T(8,128)(2,1)}), bf16[128,8192]{1,0:T(8,128)(2,1)}) %reduce-scatter.8.cloned.1.call-update) | async-done | bytes 2097168 | tf_op jit(solution)/shard_map/reduce_scatter | solution.py:67
  79.1 2.8 fusion.11
  81.9 4.3 %fusion.21 = (bf16[128,8192]{1,0:T(8,128)(2,1)}, f32[128,8192]{1,0:T(8,128)}, bf16[128,8192]{1,0:T(8,128)(2,1)}) fusion(bf16[1,128,8192]{2,1,0:T(8,128)(2,1)S(1)} %copy-done.5, f32[]{:T(128)S(6)} %convert_element_type.74, f32[128]{0:T(128)S(1)} %get-tuple-element.16, f32[128]{0:T(128)S(1)} %get-tuple-element.14, bf16[1,1,128,8192]{3,2,1,0:T(8,128)(2,1)S(1)} %copy-done.3, ...), kind=kLoop, calls=%fused_computation.41 | loop fusion | flops 14680064 | bytes 14714372 | tf_op jit(solution)/shard_map/convert_element_type | solution.py:84
  86.3 0.0 reduce-scatter.4.cloned.1.call-start
  86.3 56.8 %all-gather.2.cloned.1.call-done = bf16[256,8192]{1,0:T(8,128)(2,1)} async-done(((bf16[128,8192]{1,0:T(8,128)(2,1)}), bf16[256,8192]{1,0:T(8,128)(2,1)}) %all-gather.2.cloned.1.call-update) | async-done | bytes 4194320 | tf_op jit(solution)/shard_map/all_gather | solution.py:58
  143.2 8.2 %subtract_convert_fusion.1 = bf16[8192,512]{1,0:T(8,128)(2,1)} fusion(bf16[256,8192]{1,0:T(8,128)(2,1)} %all-gather.2.cloned.1.call-done, bf16[1,1,8192,512]{3,2,1,0:T(8,128)(2,1)} %param.16, bf16[1,1,256,512]{3,2,1,0:T(8,128)(2,1)S(1)} %copy-done), kind=kOutput, calls=%fused_computation.1 | convolution fusion | flops 2164260864 | bytes 21233664 | tf_op jit(solution)/shard_map/dot_general | solution.py:19
  151.4 8.7 %subtract_convert_fusion = bf16[8192,512]{1,0:T(8,128)(2,1)} fusion(bf16[256,8192]{1,0:T(8,128)(2,1)} %all-gather.2.cloned.1.call-done, bf16[1,1,8192,512]{3,2,1,0:T(8,128)(2,1)} %param.17, bf16[1,1,256,512]{3,2,1,0:T(8,128)(2,1)S(1)} %copy-done.7), kind=kOutput, calls=%fused_computation | convolution fusion | flops 2164260864 | bytes 21233664 | tf_op jit(solution)/shard_map/dot_general | solution.py:19
  160.1 2.1 copy-done.6
  162.3 1.3 collective-permute-start
  163.6 47.8 %collective-permute-done = bf16[128,8192]{1,0:T(8,128)(2,1)S(1)} collective-permute-done((bf16[128,8192]{1,0:T(8,128)(2,1)S(1)}, bf16[128,8192]{1,0:T(8,128)(2,1)S(1)}, u32[]{:S(2)}, u32[]{:S(2)}) %collective-permute-start) | collective-permute-done | bytes 2097184 | tf_op jit(solution)/shard_map/ppermute | solution.py:15
  211.3 2.9 add_convert_fusion.2
  214.2 1.3 collective-permute-start.1
  215.5 47.1 %collective-permute-done.1 = bf16[128,8192]{1,0:T(8,128)(2,1)S(1)} collective-permute-done((bf16[128,8192]{1,0:T(8,128)(2,1)S(1)}, bf16[128,8192]{1,0:T(8,128)(2,1)S(1)}, u32[]{:S(2)}, u32[]{:S(2)}) %collective-permute-start.1) | collective-permute-done | bytes 2097184 | tf_op jit(solution)/shard_map/ppermute | solution.py:15
  262.6 0.4 add_convert_fusion.1
  263.0 1.5 collective-permute-start.2
  264.5 46.1 %collective-permute-done.2 = bf16[128,8192]{1,0:T(8,128)(2,1)S(1)} collective-permute-done((bf16[128,8192]{1,0:T(8,128)(2,1)S(1)}, bf16[128,8192]{1,0:T(8,128)(2,1)S(1)}, u32[]{:S(2)}, u32[]{:S(2)}) %collective-permute-start.2) | collective-permute-done | bytes 2097184 | tf_op jit(solution)/shard_map/ppermute | solution.py:15
  310.6 1.8 fusion.16
  312.4 8.7 %fusion.14 = (f32[1,2048,512]{2,1,0:T(8,128)}, f32[1,2048,512]{2,1,0:T(8,128)}) fusion(bf16[2048,512]{1,0:T(8,128)(2,1)} %reduce-scatter.4.cloned.1.call-done, f32[1,2048,512]{2,1,0:T(8,128)} %param.18, f32[1,2048,512]{2,1,0:T(8,128)} %param.20), kind=kLoop, calls=%fused_computation.31 | loop fusion | flops 9437184 | bytes 18874368 | tf_op jit(solution)/shard_map/broadcast_in_dim | solution.py:106
  321.2 8.8 %fusion.15 = (f32[1,2048,512]{2,1,0:T(8,128)}, f32[1,2048,512]{2,1,0:T(8,128)}) fusion(bf16[2048,512]{1,0:T(8,128)(2,1)} %reduce-scatter.6.cloned.1.call-done, f32[1,2048,512]{2,1,0:T(8,128)} %param.19, f32[1,2048,512]{2,1,0:T(8,128)} %param.21), kind=kLoop, calls=%fused_computation.32 | loop fusion | flops 9437184 | bytes 18874368 | tf_op jit(solution)/shard_map/broadcast_in_dim | solution.py:107
  (25 shorter events, 0.3 us)
Async XLA Ops:
  7.2 1.0 copy-start
  7.2 6.7 %copy-start.7 = (bf16[1,1,256,512]{3,2,1,0:T(8,128)(2,1)S(1)}, bf16[1,1,256,512]{3,2,1,0:T(8,128)(2,1)}, u32[]{:S(2)}) copy-start(bf16[1,1,256,512]{3,2,1,0:T(8,128)(2,1)} %param.15) | copy-start | bytes 786436
  7.2 71.9 %reduce-scatter.8.cloned.1.call-start = ((), (), s32[]{:S(2)}) async-start(), calls=%async_computation.6 | async-start | bytes 6291456 | tf_op jit(solution)/shard_map/reduce_scatter | solution.py:67
  21.8 0.8 copy-start.8
  21.8 57.3 %copy-start.3 = (bf16[1,1,128,8192]{3,2,1,0:T(8,128)(2,1)S(1)}, bf16[1,1,128,8192]{3,2,1,0:T(8,128)(2,1)}, u32[]{:S(2)}) copy-start(bf16[1,1,128,8192]{3,2,1,0:T(8,128)(2,1)} %param.11) | copy-start | bytes 6291460
  21.8 121.3 %all-gather.2.cloned.1.call-start = ((), (), s32[]{:S(2)}) async-start(), calls=%async_computation.3 | async-start | bytes 6291456 | tf_op jit(solution)/shard_map/all_gather | solution.py:58
  79.1 2.8 copy-start.4
  79.1 2.9 copy-start.5
  86.3 226.1 %reduce-scatter.4.cloned.1.call-start = ((), (), s32[]{:S(2)}) async-start(), calls=%async_computation.4 | async-start | bytes 10485760 | tf_op jit(solution)/shard_map/reduce_scatter | solution.py:90
  151.4 169.8 %reduce-scatter.6.cloned.1.call-start = ((), (), s32[]{:S(2)}) async-start(), calls=%async_computation.5 | async-start | bytes 10485760 | tf_op jit(solution)/shard_map/reduce_scatter | solution.py:93
  160.1 2.2 copy-start.6
  162.3 49.1 %collective-permute-start = (bf16[128,8192]{1,0:T(8,128)(2,1)S(1)}, bf16[128,8192]{1,0:T(8,128)(2,1)S(1)}, u32[]{:S(2)}, u32[]{:S(2)}) collective-permute-start(bf16[128,8192]{1,0:T(8,128)(2,1)S(1)} %copy-done.6), channel_id=1, source_target_pairs={{2,0},{4,2},{6,4},{3,1},{5,3},{7,5},{10,8},{12,10},{14,12},{11,9},... | collective-permute-start | bytes 6291464 | tf_op jit(solution)/shard_map/ppermute | solution.py:15
  211.3 51.2 %copy-start.2 = (f32[128,8192]{1,0:T(8,128)S(1)}, f32[128,8192]{1,0:T(8,128)}, u32[]{:S(2)}) copy-start(f32[128,8192]{1,0:T(8,128)} %get-tuple-element.8) | copy-start | bytes 12582916
  214.2 48.4 %collective-permute-start.1 = (bf16[128,8192]{1,0:T(8,128)(2,1)S(1)}, bf16[128,8192]{1,0:T(8,128)(2,1)S(1)}, u32[]{:S(2)}, u32[]{:S(2)}) collective-permute-start(bf16[128,8192]{1,0:T(8,128)(2,1)S(1)} %add_convert_fusion.2), channel_id=1, source_target_pairs={{2,0},{4,2},{6,4},{3,1},{5,3},{7,5},{10,8},{12,10},{14,12},{11,9},... | collective-permute-start | bytes 6291464 | tf_op jit(solution)/shard_map/ppermute | solution.py:15
  263.0 47.6 %collective-permute-start.2 = (bf16[128,8192]{1,0:T(8,128)(2,1)S(1)}, bf16[128,8192]{1,0:T(8,128)(2,1)S(1)}, u32[]{:S(2)}, u32[]{:S(2)}) collective-permute-start(bf16[128,8192]{1,0:T(8,128)(2,1)S(1)} %add_convert_fusion.1), channel_id=1, source_target_pairs={{2,0},{4,2},{6,4},{3,1},{5,3},{7,5},{10,8},{12,10},{14,12},{11,9},... | collective-permute-start | bytes 6291464 | tf_op jit(solution)/shard_map/ppermute | solution.py:15
  321.2 8.8 %copy-start.1 = (bf16[1,1,256,512]{3,2,1,0:T(8,128)(2,1)S(1)}, bf16[1,1,256,512]{3,2,1,0:T(8,128)(2,1)}, u32[]{:S(2)}) copy-start(bf16[1,1,256,512]{3,2,1,0:T(8,128)(2,1)} %param.14) | copy-start | bytes 786436
Sparse Core Ops, SparseCore 0:
  21.9 57.0 reduce-scatter.7
  86.4 56.7 all-gather.1
  151.5 71.3 reduce-scatter.3
  225.3 71.3 reduce-scatter.5
where the time goes:
time: 337 us; the launch traced here: 336 us
  waiting for transfers between devices  254 us (75%)
  matrix products  30.5 us (9%)
  other arithmetic  29.8 us (9%)
  between operations  13.9 us (4%)
  starting transfers between devices  4.21 us (1%)
  local copies, waits for them, and re-layouts  3.77 us (1%)
    ppermute x3, waiting for transfers between devices, from_behind(): return lax.ppermute(block, axis, route)  141 us
    all_gather x1, waiting for transfers between devices, local(): piece = lax.all_gather(normed, 'tensor', axis=0, tiled=True)  56.8 us
    reduce_scatter x1, waiting for transfers between devices, local(): lax.psum_scatter(((contract_cols(key_piece, weight_key) + contract_cols(v...  56.5 us
    dot_general x2, matrix products, contract_rows(): lax.dot_general(left, right, (((0,), (0,)), ((), ())), preferred_element_...  16.9 us
    dot_general x2, matrix products, contract_cols(): lax.dot_general(left, right, (((1,), (1,)), ((), ())), preferred_element_...  13.7 us
    broadcast_in_dim x1, other arithmetic, local(): momentum_value_new[None]  8.78 us
    broadcast_in_dim x1, other arithmetic, local(): momentum_key_new[None]  8.75 us
    convert_element_type x3, other arithmetic, local(): running.astype(jnp.bfloat16)  7.59 us
  transfers between devices with their start and end apart: 7, of which 5 were waited for; matrix products, arithmetic and copies ran while one was open for 7% of the time, Pallas kernels for 0%

commit v1 on v0

v1 whole, which is shorter than its diff:
```python
import jax
import jax.numpy as jnp
from jax import lax
from jax.experimental import pallas as pl
from jax.experimental.pallas import tpu as pltpu
from jax.sharding import PartitionSpec as P

epsilon = 1e-05
inner_rate = 0.5
outer_rate = 0.7
outer_beta = 0.9


f32 = jnp.float32
bf16 = jnp.bfloat16
VMEM_LIMIT = 48 * 1024 * 1024


def spec(shape, index):
    return pl.BlockSpec(shape, index)


def call(body, grid, scalars, in_specs, out_specs, out_shape, operands, flops, aliases=None):
    moved = sum(a.size * a.dtype.itemsize for a in operands)
    moved += sum(s.size * s.dtype.itemsize for s in jax.tree.leaves(out_shape))
    return pl.pallas_call(
        body,
        grid_spec=pltpu.PrefetchScalarGridSpec(
            num_scalar_prefetch=1, grid=grid, in_specs=in_specs, out_specs=out_specs
        ),
        out_shape=out_shape,
        input_output_aliases={} if aliases is None else aliases,
        compiler_params=pltpu.CompilerParams(
            dimension_semantics=("arbitrary",) * len(grid), vmem_limit_bytes=VMEM_LIMIT
        ),
        cost_estimate=pl.CostEstimate(flops=flops, bytes_accessed=moved, transcendentals=0),
    )(scalars, *operands)


def shape(dims, kind):
    return jax.ShapeDtypeStruct(dims, kind)


def contract_rows(left, right):
    return lax.dot_general(left, right, (((0,), (0,)), ((), ())), preferred_element_type=f32)


def contract_cols(left, right):
    return lax.dot_general(left, right, (((1,), (1,)), ((), ())), preferred_element_type=f32)


def norm_kernel(island, hidden, gain, cores, chunk):
    tokens, features = hidden.shape
    outer = features // chunk // cores
    rows = min(tokens, 16)

    def body(i_ref, h_ref, g_ref, keep_ref, give_ref, inv_ref):
        core = lax.rem(i_ref[0], cores)
        resid = h_ref[...].astype(f32)
        inv = lax.rsqrt(jnp.mean(resid * resid, axis=-1, keepdims=True) + epsilon)
        inv_ref[...] = inv
        for o in range(outer):
            for ref, which in ((keep_ref, core), (give_ref, 1 - core)):
                at = pl.ds(pl.multiple_of((cores * o + which) * chunk, chunk), chunk)
                ref[:, o * chunk : (o + 1) * chunk] = (
                    h_ref[:, at].astype(f32) * inv * g_ref[:, at].astype(f32)
                ).astype(bf16)

    half = features // cores
    return call(
        body,
        (tokens // rows,),
        island,
        [spec((rows, features), lambda g, i: (g, 0)), spec((1, features), lambda g, i: (0, 0))],
        [
            spec((rows, half), lambda g, i: (g, 0)),
            spec((rows, half), lambda g, i: (g, 0)),
            spec((rows, 1), lambda g, i: (g, 0)),
        ],
        [shape((tokens, half), bf16), shape((tokens, half), bf16), shape((tokens, 1), f32)],
        [hidden, gain],
        4 * tokens * features,
    )


def partial_kernel(island, cots, weight_key, weight_value, groups, factor):
    tokens, both = cots.shape
    features, columns = weight_key.shape
    tile = min(features, 512)

    def body(i_ref, c_ref, k_ref, v_ref, *out_refs):
        part = contract_cols(c_ref[:, :columns], k_ref[...])
        part += contract_cols(c_ref[:, columns:], v_ref[...])
        part = (part * factor).astype(bf16)
        low = 0
        for ref, size in zip(out_refs, groups):
            ref[...] = part[low : low + size]
            low += size

    return call(
        body,
        (features // tile,),
        island,
        [
            spec((tokens, both), lambda g, i: (0, 0)),
            spec((tile, columns), lambda g, i: (g, 0)),
            spec((tile, columns), lambda g, i: (g, 0)),
        ],
        [spec((size, tile), lambda g, i: (0, g)) for size in groups],
        [shape((size, features), bf16) for size in groups],
        [cots, weight_key, weight_value],
        2 * tokens * features * both,
    )


class Rows:
    def __init__(self, cores, outers, chunk, tile, turn, start):
        self.cores, self.outers, self.per, self.turn, self.first = (
            cores,
            outers,
            chunk // tile,
            turn,
            start // tile,
        )

    def outer(self, i):
        return lax.rem(i[0] // self.cores + self.turn, self.outers)

    def of_weights(self, g, i):
        core = lax.rem(i[0], self.cores)
        return (self.outer(i) * self.cores + core) * self.per + self.first + g

    def of_half(self, g, i):
        return self.outer(i) * self.per + self.first + g


def product(mine, theirs, cots):
    total, low = None, 0
    for block in mine + theirs:
        high = low + block.shape[0]
        part = contract_rows(block[...], cots[low:high])
        total = part if total is None else total + part
        low = high
    return total


def delta_specs(rows, first, tile, pair, remote, cots, columns):
    specs = [spec((p.shape[0], tile), lambda g, i: (0, rows.of_half(g, i))) for p in pair]
    specs += [spec((p.shape[0], tile), lambda g, i: (0, first + g)) for p in remote]
    specs += [spec(cots.shape, lambda g, i: (0, 0))]
    specs += [spec((tile, columns), lambda g, i: (rows.of_weights(g, i), 0))] * 2
    return specs


def send_kernel(island, rows, count, tile, pair, remote, cots, weights, got, rate):
    columns = weights[0].shape[1]
    n_pair, n_all = len(pair), len(pair) + len(remote)
    per = rows.first

    def body(i_ref, *refs):
        parts = product(list(refs[:n_pair]), list(refs[n_pair:n_all]), refs[n_all])
        wk, wv, got_ref, out_ref = refs[n_all + 1 :]
        for at, w in ((0, wk), (1, wv)):
            low = at * columns
            base = w[...].astype(f32) + got_ref[at].astype(f32)
            out_ref[:, low : low + columns] = (
                base - rate * parts[:, low : low + columns]
            ).astype(bf16)

    return call(
        body,
        (count // tile,),
        island,
        delta_specs(rows, 0, tile, pair, remote, cots, columns)
        + [spec((2, tile, columns), lambda g, i: (0, per + g, 0))],
        spec((tile, 2 * columns), lambda g, i: (g, 0)),
        shape((count, 2 * columns), bf16),
        [*pair, *remote, cots, *weights, got],
        2 * count * cots.shape[0] * 2 * columns,
    )


def update_kernel(
    island, rows, count, tile, pair, remote, first, cots, weights, got, arrived, state, done, rate, islands
):
    columns = weights[0].shape[1]
    n_pair, n_all = len(pair), len(pair) + len(remote)
    n_in = n_all + 4 + len(arrived) + 4
    per = rows.first
    n_done = 0 if done is None else 4

    def body(i_ref, *refs):
        parts = product(list(refs[:n_pair]), list(refs[n_pair:n_all]), refs[n_all])
        weight_refs, got_ref = refs[n_all + 1 : n_all + 3], refs[n_all + 3]
        come = refs[n_all + 4 : n_all + 4 + len(arrived)]
        anchors = refs[n_in - 4 : n_in - 2]
        momenta = refs[n_in - 2 : n_in]
        outs = refs[n_in + n_done :]
        for at in range(2):
            low = at * columns
            total = weight_refs[at][...].astype(f32) + got_ref[at].astype(f32)
            total -= rate * parts[:, low : low + columns]
            for ref in come:
                total += ref[:, low : low + columns].astype(f32)
            anchor = anchors[at][...]
            mean = anchor - total / islands
            momentum = outer_beta * momenta[at][...] + mean
            outs[at][...] = anchor - outer_rate * (mean + outer_beta * momentum)
            outs[2 + at][...] = momentum

    whole = state[0].shape
    own = spec((tile, columns), lambda g, i: (per + g, 0))
    specs = (
        delta_specs(rows, first // tile, tile, pair, remote, cots, columns)
        + [spec((2, tile, columns), lambda g, i: (0, per + g, 0))]
        + [spec((tile, 2 * columns), lambda g, i: (g, 0))] * len(arrived)
        + [own] * 4
    )
    operands = [*pair, *remote, cots, *weights, got, *arrived, *state]
    aliases = {}
    if done is not None:
        specs += [pl.BlockSpec(memory_space=pl.ANY)] * 4
        aliases = {1 + len(operands) + k: k for k in range(4)}
        operands += list(done)
    return call(
        body,
        (count // tile,),
        island,
        specs,
        [own] * 4,
        [shape(whole, f32)] * 4,
        operands,
        2 * count * cots.shape[0] * 2 * columns,
        aliases,
    )


def branch_kernel(start, count, hidden, gain, inv, own, parts, above, top):
    features = hidden.shape[1]
    rows = min(count, 16)
    base = start // rows
    n_parts = len(parts)

    def body(t_ref, h_ref, g_ref, inv_ref, own_ref, *refs):
        above_ref, out_ref, out16_ref = refs[n_parts:]
        upstream = own_ref[...].astype(f32)
        for ref in refs[:n_parts]:
            upstream += ref[...].astype(f32)
        scaled = g_ref[...].astype(f32) * upstream
        resid = h_ref[...].astype(f32)
        inv_rms = inv_ref[...]
        mean = jnp.mean(resid * scaled, axis=-1, keepdims=True)
        is_top = (t_ref[0] == 1).astype(f32)
        term = inv_rms * scaled - resid * (inv_rms * inv_rms * inv_rms * mean)
        term += is_top * above_ref[...].astype(f32)
        out_ref[...] = term
        out16_ref[...] = term.astype(bf16)

    own_rows = spec((rows, features), lambda g, i: (base + g, 0))
    part_rows = spec((rows, features), lambda g, i: (g, 0))
    return call(
        body,
        (count // rows,),
        top,
        [
            own_rows,
            spec((1, features), lambda g, i: (0, 0)),
            spec((rows, 1), lambda g, i: (base + g, 0)),
            own_rows,
            *[part_rows] * n_parts,
            own_rows,
        ],
        [part_rows, part_rows],
        [shape((count, features), f32), shape((count, features), bf16)],
        [hidden, gain, inv, own, *parts, above],
        8 * count * features,
    )


def final_kernel(island, start, tokens, term, arrived, done):
    count, features = term.shape
    rows = min(count, 16)
    base = start // rows

    def body(i_ref, term_ref, *refs):
        total = term_ref[...]
        for ref in refs[: len(arrived)]:
            total += ref[...].astype(f32)
        refs[-1][...] = total.astype(bf16)

    part_rows = spec((rows, features), lambda g, i: (g, 0))
    specs = [part_rows] * (1 + len(arrived))
    operands = [term, *arrived]
    aliases = {}
    if done is not None:
        specs.append(pl.BlockSpec(memory_space=pl.ANY))
        aliases = {1 + len(operands): 0}
        operands.append(done)
    return call(
        body,
        (count // rows,),
        island,
        specs,
        spec((rows, features), lambda g, i: (base + g, 0)),
        shape((tokens, features), bf16),
        operands,
        4 * count * features,
        aliases,
    )


def move(block, axis, target):
    size = lax.axis_size(axis)
    route = [(i, target(i)) for i in range(size) if target(i) is not None]
    return lax.ppermute(block, axis, route)


def local(
    hidden,
    norm_gain,
    grad_above,
    key_cot,
    value_cot,
    local_key,
    local_value,
    anchor_key,
    anchor_value,
    momentum_key,
    momentum_value,
):
    islands, sections, tensors = (lax.axis_size(a) for a in ("island", "section", "tensor"))
    cores = 2
    outers = islands // cores
    island = lax.axis_index("island")
    section = lax.axis_index("section")
    tensor = lax.axis_index("tensor")
    core, outer = island % cores, island // cores
    scalars = island.astype(jnp.int32).reshape(1)
    top = (section == sections - 1).astype(jnp.int32).reshape(1)

    resid, above = hidden[0, 0], grad_above[0]
    weights = [local_key[0, 0], local_value[0, 0]]
    tokens, features = resid.shape
    columns = weights[0].shape[1]
    factor = float(features) ** (-0.5)
    owned = features // islands
    state = [a[0] for a in (anchor_key, anchor_value, momentum_key, momentum_value)]

    def across(i):
        return i - i % cores + (cores - 1 - i % cores)

    cot = jnp.concatenate([key_cot[0, 0], value_cot[0, 0]], axis=1)
    cot = cot.reshape(tensors, tokens, 2 * columns)
    cots = jnp.concatenate(
        [
            lax.dynamic_index_in_dim(cot, (tensor + e) % tensors, 0, keepdims=False)
            for e in range(tensors)
        ]
    )
    cots_other = move(cots, "island", across)
    order = []
    for e in range(tensors):
        for c in (cots, cots_other):
            order.append(c[e * tokens : (e + 1) * tokens])
    all_cots = jnp.concatenate(order)

    got = []
    for turn in list(range(1, outers)) + [0]:
        block = jnp.stack(
            [
                lax.dynamic_slice_in_dim(
                    w,
                    (((outer + turn) % outers) * cores + (cores - 1 - core)) * owned,
                    owned,
                )
                for w in weights
            ]
        )
        got.append(move(block, "island", across))
    got = [got[-1], *got[:-1]]

    keep, give, inv = norm_kernel(scalars, resid, norm_gain, cores, owned)
    other = move(give, "island", across)
    pair = [keep, other]

    n_rows = 4
    n_tokens = max(1, min(4, tokens // 16))
    row_chunk, token_chunk = owned // n_rows, tokens // n_tokens

    def gather(turn, start, count):
        low = ((outer + turn) % outers) * owned + start
        block = jnp.concatenate([lax.dynamic_slice_in_dim(p, low, count, axis=1) for p in pair])
        come = []
        for e in range(1, tensors):
            come.append(move(block, "tensor", lambda i: (i - e) % tensors))
        return come

    groups = [tokens] + [token_chunk] * (n_tokens * (tensors - 1))
    partials = partial_kernel(scalars, cots, *weights, groups, factor)
    own_part, parts = partials[0], partials[1:]
    tile = min(row_chunk, 256)

    sent = {}
    for q in range(n_rows):
        for turn in range(1, outers):
            remote = gather(turn, q * row_chunk, row_chunk)
            rows = Rows(cores, outers, owned, tile, turn, q * row_chunk)
            block = send_kernel(
                scalars,
                rows,
                row_chunk,
                tile,
                pair,
                remote,
                all_cots,
                weights,
                got[turn],
                inner_rate * factor,
            )
            sent[q, turn] = move(
                block, "island", lambda i: (i + turn * cores) % islands
            )

    input_grad = None
    for q in range(n_tokens):
        arrived = []
        for e in range(1, tensors):
            arrived.append(
                move(
                    parts[(e - 1) * n_tokens + q],
                    "tensor",
                    lambda i: (i + e) % tensors,
                )
            )
        term, rounded = branch_kernel(
            q * token_chunk, token_chunk, resid, norm_gain, inv, own_part, arrived, above, top
        )
        hops = []
        for hop in range(sections - 1):
            if hop:
                running = term
                for come in hops:
                    running = running + come.astype(f32)
                rounded = running.astype(bf16)
            hops.append(
                move(
                    rounded,
                    "section",
                    lambda i: i - 1 if i == sections - 1 - hop else None,
                )
            )
        input_grad = final_kernel(scalars, q * token_chunk, tokens, term, hops, input_grad)

    outs = None
    n_own = 2
    own_chunk = owned // n_own
    for q in range(n_rows):
        if q % (n_rows // n_own) == 0:
            remote = gather(0, q * row_chunk, own_chunk)
        rows = Rows(cores, outers, owned, tile, 0, q * row_chunk)
        outs = update_kernel(
            scalars,
            rows,
            row_chunk,
            tile,
            pair,
            remote,
            (q % (n_rows // n_own)) * row_chunk,
            all_cots,
            weights,
            got[0],
            [sent[q, turn] for turn in range(1, outers)],
            state,
            outs,
            inner_rate * factor,
            islands,
        )
    return (*[o[None] for o in outs], input_grad[None, None])


def solution(mesh):
    placed = (
        P("island", "section", "tensor", None),
        P("section", None),
        P("island", "tensor", None),
        P("island", "section", None, "tensor"),
        P("island", "section", None, "tensor"),
        P("island", "section", None, "tensor"),
        P("island", "section", None, "tensor"),
        P("section", "island", "tensor"),
        P("section", "island", "tensor"),
        P("section", "island", "tensor"),
        P("section", "island", "tensor"),
    )

    return jax.shard_map(
        local,
        mesh=mesh,
        in_specs=placed,
        out_specs=(
            P("section", "island", "tensor"),
            P("section", "island", "tensor"),
            P("section", "island", "tensor"),
            P("section", "island", "tensor"),
            P("island", "section", "tensor", None),
        ),
        check_vma=False,
    )
```

time: 337 us -> 265 us (0.79)
  waiting for transfers between devices: 254 us -> 140 us
  Pallas kernels: 0 us -> 63.8 us
  matrix products: 30.5 us -> 0 us
  starting transfers between devices: 4.21 us -> 31.1 us
  other arithmetic: 29.8 us -> 14.2 us
  between operations: 13.9 us -> 1.15 us
  local copies, waits for them, and re-layouts: 3.77 us -> 12.1 us
    pallas_call x0 -> x18, Pallas kernels: none -> 63.8 us  [call(): pl.pallas_call(body, grid_spec=pltpu.PrefetchScalarGridSpec(num_scalar_pr...]
    all_gather x1 -> x0, waiting for transfers between devices: 56.8 us -> none  [local(): piece = lax.all_gather(normed, 'tensor', axis=0, tiled=True)]
    reduce_scatter x3 -> x0, waiting for transfers between devices: 56.5 us -> none  [the longest x1 56.5 us: local(): lax.psum_scatter(((contract_cols(key_piece, weight_key) + contract_cols(v...]
    dot_general x4 -> x0, matrix products: 30.5 us -> none  [the longest x2 16.9 us: contract_rows(): lax.dot_general(left, right, (((0,), (0,)), ((), ())), preferred_element_...]
    ppermute x3 -> x30, starting transfers between devices: 4.04 us -> 31.1 us  [move(): return lax.ppermute(block, axis, route)]
    broadcast_in_dim x3 -> x0, other arithmetic: 19.3 us -> none  [the longest x1 8.78 us: local(): momentum_value_new[None]]
    another operation x0 -> x2, other arithmetic: none -> 8.61 us  [local(): jnp.stack([lax.dynamic_slice_in_dim(w, ((outer + turn) % outers * cores +...]
    another operation x0 -> x1, local copies, waits for them, and re-layouts: none -> 7.07 us  [local(): jnp.stack([lax.dynamic_slice_in_dim(w, ((outer + turn) % outers * cores +...]
  transfers between devices with their start and end apart: 7 -> 30, of which waited for: 5 -> 15; matrix products, arithmetic and copies ran while one was open for 7% -> 9% of each run, Pallas kernels for 0% -> 22%
where the time goes in v1:
time: 265 us; the launch traced here: 262 us
  waiting for transfers between devices  140 us (53%)
  Pallas kernels  63.8 us (24%)
  starting transfers between devices  31.1 us (12%)
  other arithmetic  14.2 us (5%)
  local copies, waits for them, and re-layouts  12.1 us (5%)
    ppermute x30, waiting for transfers between devices, move(): return lax.ppermute(block, axis, route)  140 us
    pallas_call x18, Pallas kernels, call(): pl.pallas_call(body, grid_spec=pltpu.PrefetchScalarGridSpec(num_scalar_pr...  63.8 us
    ppermute x30, starting transfers between devices, move(): return lax.ppermute(block, axis, route)  31.1 us
    another operation x2, other arithmetic, local(): jnp.stack([lax.dynamic_slice_in_dim(w, ((outer + turn) % outers * cores +...  8.61 us
    another operation x1, local copies, waits for them, and re-layouts, local(): jnp.stack([lax.dynamic_slice_in_dim(w, ((outer + turn) % outers * cores +...  7.07 us
  transfers between devices with their start and end apart: 30, of which 15 were waited for; matrix products, arithmetic and copies ran while one was open for 9% of the time, Pallas kernels for 22%

profile of v1, /device:TPU:0, one launch (start us, length us, event | category | flops | bytes accessed | tf_op | source)
XLA Modules:
  0.0 262.4 jit_solution(11381970012351798480)
XLA Ops:
  3.1 15.6 %shard_map.155 = (bf16[128,8192]{1,0:T(8,128)(2,1)S(1)}, bf16[32,8192]{1,0:T(8,128)(2,1)}, bf16[32,8192]{1,0:T(8,128)(2,1)}, bf16[32,8192]{1,0:T(8,128)(2,1)}, bf16[32,8192]{1,0:T(8,128)(2,1)}) custom-call(s32[1]{0:T(128)} %bitcast.i_ref, bf16[256,1024]{1,0:T(8,128)(2,1)S(1)} %pad_maximum_fusion.4.c_ref, bf16[8192,512]{1,0:T(8,128)(2,1)} %bitcast.34, ...), custom_call_target="tpu_custom_call" | custom-call | flops 4294967296 | bytes 21495808 | tf_op jit(solution)/shard_map/pallas_call | solution.py:26
  24.6 7.1 %dynamic-slice_bitcast_fusion = (bf16[1,2048,512]{2,1,0:T(8,128)(2,1)}, bf16[1,2048,512]{2,1,0:T(8,128)(2,1)}, bf16[1,2048,512]{2,1,0:T(8,128)(2,1)}, bf16[1,2048,512]{2,1,0:T(8,128)(2,1)}) fusion(bf16[1,1,8192,512]{3,2,1,0:T(8,128)(2,1)} %param.17, s32[]{:T(128)S(6)} %select_n.93, s32[]{:T(128)S(6)} %select_n.90, bf16[1,1,8192,512]{3,2,1,0:T(8,128)(2,1)} %param.16), kind=kLoop, calls=%fused_computation.2 | loop fusion | bytes 16777224 | tf_op jit(solution)/shard_map/stack | solution.py:369
  33.5 4.6 %pad_maximum_fusion = bf16[2,2048,512]{2,1,0:T(8,128)(2,1)} fusion(bf16[1,2048,512]{2,1,0:T(8,128)(2,1)} %get-tuple-element.72, bf16[1,2048,512]{2,1,0:T(8,128)(2,1)} %get-tuple-element.89), kind=kLoop, calls=%fused_computation | loop fusion | flops 2097152 | bytes 8388608 | tf_op jit(solution)/shard_map/stack | solution.py:369
  41.9 4.0 %pad_maximum_fusion.1 = bf16[2,2048,512]{2,1,0:T(8,128)(2,1)} fusion(bf16[1,2048,512]{2,1,0:T(8,128)(2,1)S(1)} %copy-done.9, bf16[1,2048,512]{2,1,0:T(8,128)(2,1)} %get-tuple-element.90), kind=kLoop, calls=%fused_computation.1 | loop fusion | flops 2097152 | bytes 8388608 | tf_op jit(solution)/shard_map/stack | solution.py:369
  49.0 9.2 %collective-permute-done.22.refs_0_ = bf16[32,8192]{1,0:T(8,128)(2,1)} collective-permute-done((bf16[32,8192]{1,0:T(8,128)(2,1)}, bf16[32,8192]{1,0:T(8,128)(2,1)}, u32[]{:S(2)}, u32[]{:S(2)}) %collective-permute-start.22) | collective-permute-done | bytes 524320 | tf_op jit(solution)/shard_map/ppermute | solution.py:315
  60.2 8.9 %collective-permute-done.26.refs_0_ = bf16[32,8192]{1,0:T(8,128)(2,1)S(1)} collective-permute-done((bf16[32,8192]{1,0:T(8,128)(2,1)}, bf16[32,8192]{1,0:T(8,128)(2,1)S(1)}, u32[]{:S(2)}, u32[]{:S(2)}) %collective-permute-start.26) | collective-permute-done | bytes 524320 | tf_op jit(solution)/shard_map/ppermute | solution.py:315
  84.3 3.9 %collective-permute-done.7.refs_2_ = bf16[256,512]{1,0:T(8,128)(2,1)S(1)} collective-permute-done((bf16[256,512]{1,0:T(8,128)(2,1)S(1)}, bf16[256,512]{1,0:T(8,128)(2,1)S(1)}, u32[]{:S(2)}, u32[]{:S(2)}) %collective-permute-start.7) | collective-permute-done | bytes 262176 | tf_op jit(solution)/shard_map/ppermute | solution.py:315
  95.6 3.9 %collective-permute-done.12.refs_2_ = bf16[256,512]{1,0:T(8,128)(2,1)S(1)} collective-permute-done((bf16[256,512]{1,0:T(8,128)(2,1)S(1)}, bf16[256,512]{1,0:T(8,128)(2,1)S(1)}, u32[]{:S(2)}, u32[]{:S(2)}) %collective-permute-start.12) | collective-permute-done | bytes 262176 | tf_op jit(solution)/shard_map/ppermute | solution.py:315
  103.0 6.6 %collective-permute-done.9.refs_2_ = bf16[256,1024]{1,0:T(8,128)(2,1)S(1)} collective-permute-done((bf16[256,1024]{1,0:T(8,128)(2,1)S(1)}, bf16[256,1024]{1,0:T(8,128)(2,1)S(1)}, u32[]{:S(2)}, u32[]{:S(2)}) %collective-permute-start.9) | collective-permute-done | bytes 524320 | tf_op jit(solution)/shard_map/ppermute | solution.py:315
  113.5 3.4 %shard_map.150 = bf16[512,1024]{1,0:T(8,128)(2,1)} custom-call(s32[1]{0:T(128)} %bitcast.i_ref, bf16[128,4096]{1,0:T(8,128)(2,1)S(1)} %get-tuple-element.37.refs_0_, bf16[128,4096]{1,0:T(8,128)(2,1)S(1)} %collective-permute-done.refs_1_, bf16[256,512]{1,0:T(8,128)(2,1)S(1)} %collective-permute-done.12.refs_2_, ...), custom_call_target="tpu_custom_call" | custom-call | flops 536870912 | bytes 25427968 | tf_op jit(solution)/shard_map/pallas_call | solution.py:26
  116.9 50.8 %collective-permute-done.17.refs_2_ = bf16[32,8192]{1,0:T(8,128)(2,1)S(1)} collective-permute-done((bf16[32,8192]{1,0:T(8,128)(2,1)}, bf16[32,8192]{1,0:T(8,128)(2,1)S(1)}, u32[]{:S(2)}, u32[]{:S(2)}) %collective-permute-start.17) | collective-permute-done | bytes 524320 | tf_op jit(solution)/shard_map/ppermute | solution.py:315
  169.2 3.3 %shard_map.149 = bf16[512,1024]{1,0:T(8,128)(2,1)} custom-call(s32[1]{0:T(128)} %bitcast.i_ref, bf16[128,4096]{1,0:T(8,128)(2,1)S(1)} %get-tuple-element.37.refs_0_, bf16[128,4096]{1,0:T(8,128)(2,1)S(1)} %collective-permute-done.refs_1_, bf16[256,512]{1,0:T(8,128)(2,1)S(1)} %collective-permute-done.10.refs_2_, ...), custom_call_target="tpu_custom_call" | custom-call | flops 536870912 | bytes 25427968 | tf_op jit(solution)/shard_map/pallas_call | solution.py:26
  172.5 6.4 %collective-permute-done.21.refs_2_ = bf16[32,8192]{1,0:T(8,128)(2,1)S(1)} collective-permute-done((bf16[32,8192]{1,0:T(8,128)(2,1)}, bf16[32,8192]{1,0:T(8,128)(2,1)S(1)}, u32[]{:S(2)}, u32[]{:S(2)}) %collective-permute-start.21) | collective-permute-done | bytes 524320 | tf_op jit(solution)/shard_map/ppermute | solution.py:315
  180.4 3.3 %shard_map.148 = bf16[512,1024]{1,0:T(8,128)(2,1)} custom-call(s32[1]{0:T(128)} %bitcast.i_ref, bf16[128,4096]{1,0:T(8,128)(2,1)S(1)} %get-tuple-element.37.refs_0_, bf16[128,4096]{1,0:T(8,128)(2,1)S(1)} %collective-permute-done.refs_1_, bf16[256,512]{1,0:T(8,128)(2,1)S(1)} %collective-permute-done.7.refs_2_, ...), custom_call_target="tpu_custom_call" | custom-call | flops 536870912 | bytes 25427968 | tf_op jit(solution)/shard_map/pallas_call | solution.py:26
  183.7 6.4 %collective-permute-done.25.refs_2_ = bf16[32,8192]{1,0:T(8,128)(2,1)S(1)} collective-permute-done((bf16[32,8192]{1,0:T(8,128)(2,1)}, bf16[32,8192]{1,0:T(8,128)(2,1)S(1)}, u32[]{:S(2)}, u32[]{:S(2)}) %collective-permute-start.25) | collective-permute-done | bytes 524320 | tf_op jit(solution)/shard_map/ppermute | solution.py:315
  191.6 3.3 %shard_map.147 = bf16[512,1024]{1,0:T(8,128)(2,1)} custom-call(s32[1]{0:T(128)} %bitcast.i_ref, bf16[128,4096]{1,0:T(8,128)(2,1)S(1)} %get-tuple-element.37.refs_0_, bf16[128,4096]{1,0:T(8,128)(2,1)S(1)} %collective-permute-done.refs_1_, bf16[256,512]{1,0:T(8,128)(2,1)S(1)} %collective-permute-done.4.refs_2_, ...), custom_call_target="tpu_custom_call" | custom-call | flops 536870912 | bytes 25427968 | tf_op jit(solution)/shard_map/pallas_call | solution.py:26
  195.0 4.8 %collective-permute-done.29.refs_2_ = bf16[32,8192]{1,0:T(8,128)(2,1)S(1)} collective-permute-done((bf16[32,8192]{1,0:T(8,128)(2,1)}, bf16[32,8192]{1,0:T(8,128)(2,1)S(1)}, u32[]{:S(2)}, u32[]{:S(2)}) %collective-permute-start.29) | collective-permute-done | bytes 524320 | tf_op jit(solution)/shard_map/ppermute | solution.py:315
  207.0 5.3 %shard_map.151 = (f32[2048,512]{1,0:T(8,128)}, f32[2048,512]{1,0:T(8,128)}, f32[2048,512]{1,0:T(8,128)}, f32[2048,512]{1,0:T(8,128)}) custom-call(s32[1]{0:T(128)} %bitcast.i_ref, bf16[128,4096]{1,0:T(8,128)(2,1)S(1)} %get-tuple-element.37.refs_0_, bf16[128,4096]{1,0:T(8,128)(2,1)S(1)} %collective-permute-done.refs_1_, ...), custom_call_target="tpu_custom_call" | custom-call | flops 536870912 | bytes 59244544 | tf_op jit(solution)/shard_map/pallas_call | solution.py:26
  212.3 4.2 %collective-permute-done.11.refs_7_ = bf16[512,1024]{1,0:T(8,128)(2,1)} collective-permute-done((bf16[512,1024]{1,0:T(8,128)(2,1)}, bf16[512,1024]{1,0:T(8,128)(2,1)}, u32[]{:S(2)}, u32[]{:S(2)}) %collective-permute-start.11) | collective-permute-done | bytes 1048608 | tf_op jit(solution)/shard_map/ppermute | solution.py:315
  216.5 5.3 %shard_map.152 = (f32[2048,512]{1,0:T(8,128)}, f32[2048,512]{1,0:T(8,128)}, f32[2048,512]{1,0:T(8,128)}, f32[2048,512]{1,0:T(8,128)}) custom-call(s32[1]{0:T(128)} %bitcast.i_ref, bf16[128,4096]{1,0:T(8,128)(2,1)S(1)} %get-tuple-element.37.refs_0_, ...), custom_call_target="tpu_custom_call", output_to_operand_aliasing={{0}: (13, {}), {1}: (14, {}), {2}: (15, {}), {3}: (16, {})} | custom-call | flops 536870912 | bytes 76021760 | tf_op jit(solution)/shard_map/pallas_call | solution.py:26
  221.8 17.1 %collective-permute-done.8.refs_7_ = bf16[512,1024]{1,0:T(8,128)(2,1)} collective-permute-done((bf16[512,1024]{1,0:T(8,128)(2,1)}, bf16[512,1024]{1,0:T(8,128)(2,1)}, u32[]{:S(2)}, u32[]{:S(2)}) %collective-permute-start.8) | collective-permute-done | bytes 1048608 | tf_op jit(solution)/shard_map/ppermute | solution.py:315
  238.9 5.3 %shard_map.153 = (f32[2048,512]{1,0:T(8,128)}, f32[2048,512]{1,0:T(8,128)}, f32[2048,512]{1,0:T(8,128)}, f32[2048,512]{1,0:T(8,128)}) custom-call(s32[1]{0:T(128)} %bitcast.i_ref, bf16[128,4096]{1,0:T(8,128)(2,1)S(1)} %get-tuple-element.37.refs_0_, ...), custom_call_target="tpu_custom_call", output_to_operand_aliasing={{0}: (13, {}), {1}: (14, {}), {2}: (15, {}), {3}: (16, {})} | custom-call | flops 536870912 | bytes 76021760 | tf_op jit(solution)/shard_map/pallas_call | solution.py:26
  244.3 12.9 %collective-permute-done.6.refs_7_ = bf16[512,1024]{1,0:T(8,128)(2,1)S(1)} collective-permute-done((bf16[512,1024]{1,0:T(8,128)(2,1)}, bf16[512,1024]{1,0:T(8,128)(2,1)S(1)}, u32[]{:S(2)}, u32[]{:S(2)}) %collective-permute-start.6) | collective-permute-done | bytes 1048608 | tf_op jit(solution)/shard_map/ppermute | solution.py:315
  257.2 5.1 %shard_map.154 = (f32[2048,512]{1,0:T(8,128)}, f32[2048,512]{1,0:T(8,128)}, f32[2048,512]{1,0:T(8,128)}, f32[2048,512]{1,0:T(8,128)}) custom-call(s32[1]{0:T(128)} %bitcast.i_ref, bf16[128,4096]{1,0:T(8,128)(2,1)S(1)} %get-tuple-element.37.refs_0_, ...), custom_call_target="tpu_custom_call", output_to_operand_aliasing={{0}: (13, {}), {1}: (14, {}), {2}: (15, {}), {3}: (16, {})} | custom-call | flops 536870912 | bytes 76021760 | tf_op jit(solution)/shard_map/pallas_call | solution.py:26
  (107 shorter events, 60.7 us)
Async XLA Ops:
  2.5 78.3 %collective-permute-start.2 = (bf16[256,1024]{1,0:T(8,128)(2,1)S(1)}, bf16[256,1024]{1,0:T(8,128)(2,1)}, u32[]{:S(2)}, u32[]{:S(2)}) collective-permute-start(bf16[256,1024]{1,0:T(8,128)(2,1)S(1)} %pad_maximum_fusion.4.c_ref), channel_id=1, source_target_pairs={{0,8},{8,0},{16,24},{24,16},{1,9},{9,1},{17,25},{25,17},{2,10},{10... | collective-permute-start | bytes 1572872 | tf_op jit(solution)/shard_map/ppermute | solution.py:315
  20.1 18.1 %collective-permute-start.14 = (bf16[32,8192]{1,0:T(8,128)(2,1)}, bf16[32,8192]{1,0:T(8,128)(2,1)}, u32[]{:S(2)}, u32[]{:S(2)}) collective-permute-start(bf16[32,8192]{1,0:T(8,128)(2,1)} %get-tuple-element.57), channel_id=1, source_target_pairs={{0,1},{1,0},{2,3},{3,2},{4,5},{5,4},{6,7},{7,6},{8,9},{9,8},{10,11... | collective-permute-start | bytes 1572872 | tf_op jit(solution)/shard_map/ppermute | solution.py:315
  22.6 24.3 %collective-permute-start.18 = (bf16[32,8192]{1,0:T(8,128)(2,1)}, bf16[32,8192]{1,0:T(8,128)(2,1)}, u32[]{:S(2)}, u32[]{:S(2)}) collective-permute-start(bf16[32,8192]{1,0:T(8,128)(2,1)} %get-tuple-element.60), channel_id=1, source_target_pairs={{0,1},{1,0},{2,3},{3,2},{4,5},{5,4},{6,7},{7,6},{8,9},{9,8},{10,11... | collective-permute-start | bytes 1572872 | tf_op jit(solution)/shard_map/ppermute | solution.py:315
  22.6 35.5 %collective-permute-start.22 = (bf16[32,8192]{1,0:T(8,128)(2,1)}, bf16[32,8192]{1,0:T(8,128)(2,1)}, u32[]{:S(2)}, u32[]{:S(2)}) collective-permute-start(bf16[32,8192]{1,0:T(8,128)(2,1)} %get-tuple-element.63), channel_id=1, source_target_pairs={{0,1},{1,0},{2,3},{3,2},{4,5},{5,4},{6,7},{7,6},{8,9},{9,8},{10,11... | collective-permute-start | bytes 1572872 | tf_op jit(solution)/shard_map/ppermute | solution.py:315
  24.6 44.4 %collective-permute-start.26 = (bf16[32,8192]{1,0:T(8,128)(2,1)}, bf16[32,8192]{1,0:T(8,128)(2,1)S(1)}, u32[]{:S(2)}, u32[]{:S(2)}) collective-permute-start(bf16[32,8192]{1,0:T(8,128)(2,1)} %get-tuple-element.66), channel_id=1, source_target_pairs={{0,1},{1,0},{2,3},{3,2},{4,5},{5,4},{6,7},{7,6},{8,9},{9,8},{10,11... | collective-permute-start | bytes 1572872 | tf_op jit(solution)/shard_map/ppermute | solution.py:315
  40.4 31.4 %collective-permute-start.15 = (bf16[32,8192]{1,0:T(8,128)(2,1)S(1)}, bf16[32,8192]{1,0:T(8,128)(2,1)S(1)}, u32[]{:S(2)}, u32[]{:S(2)}) collective-permute-start(bf16[32,8192]{1,0:T(8,128)(2,1)S(1)} %get-tuple-element.59), channel_id=1, source_target_pairs={{6,4},{7,5},{14,12},{15,13},{22,20},{23,21},{30,28},{31,29}} | collective-permute-start | bytes 1572872 | tf_op jit(solution)/shard_map/ppermute | solution.py:315
  46.9 25.6 %collective-permute-start = (bf16[128,4096]{1,0:T(8,128)(2,1)S(1)}, bf16[128,4096]{1,0:T(8,128)(2,1)S(1)}, u32[]{:S(2)}, u32[]{:S(2)}) collective-permute-start(bf16[128,4096]{1,0:T(8,128)(2,1)S(1)} %get-tuple-element.38), channel_id=1, source_target_pairs={{0,8},{8,0},{16,24},{24,16},{1,9},{9,1},{17,25},{25,17},{2,10},{10... | collective-permute-start | bytes 3145736 | tf_op jit(solution)/shard_map/ppermute | solution.py:315
  58.1 52.7 %collective-permute-start.5 = (bf16[2,2048,512]{2,1,0:T(8,128)(2,1)}, bf16[2,2048,512]{2,1,0:T(8,128)(2,1)}, u32[]{:S(2)}, u32[]{:S(2)}) collective-permute-start(bf16[2,2048,512]{2,1,0:T(8,128)(2,1)} %pad_maximum_fusion.1), channel_id=1, source_target_pairs={{0,8},{8,0},{16,24},{24,16},{1,9},{9,1},{17,25},{25,17},{2,10},{10... | collective-permute-start | bytes 12582920 | tf_op jit(solution)/shard_map/ppermute | solution.py:315
  75.3 12.9 %collective-permute-start.7 = (bf16[256,512]{1,0:T(8,128)(2,1)S(1)}, bf16[256,512]{1,0:T(8,128)(2,1)S(1)}, u32[]{:S(2)}, u32[]{:S(2)}) collective-permute-start(bf16[256,512]{1,0:T(8,128)(2,1)S(1)} %pad_maximum_fusion.7), channel_id=1, source_target_pairs={{0,1},{1,0},{2,3},{3,2},{4,5},{5,4},{6,7},{7,6},{8,9},{9,8},{10,11... | collective-permute-start | bytes 786440 | tf_op jit(solution)/shard_map/ppermute | solution.py:315
  79.1 10.9 %collective-permute-start.24 = (bf16[32,8192]{1,0:T(8,128)(2,1)S(1)}, bf16[32,8192]{1,0:T(8,128)(2,1)S(1)}, u32[]{:S(2)}, u32[]{:S(2)}) collective-permute-start(bf16[32,8192]{1,0:T(8,128)(2,1)S(1)} %fusion.2), channel_id=1, source_target_pairs={{4,2},{5,3},{12,10},{13,11},{20,18},{21,19},{28,26},{29,27}} | collective-permute-start | bytes 1572872 | tf_op jit(solution)/shard_map/ppermute | solution.py:315
  80.8 120.5 %collective-permute-start.3 = (bf16[2,2048,512]{2,1,0:T(8,128)(2,1)}, bf16[2,2048,512]{2,1,0:T(8,128)(2,1)}, u32[]{:S(2)}, u32[]{:S(2)}) collective-permute-start(bf16[2,2048,512]{2,1,0:T(8,128)(2,1)} %pad_maximum_fusion), channel_id=1, source_target_pairs={{0,8},{8,0},{16,24},{24,16},{1,9},{9,1},{17,25},{25,17},{2,10},{10... | collective-permute-start | bytes 12582920 | tf_op jit(solution)/shard_map/ppermute | solution.py:315
  82.6 11.2 %collective-permute-start.10 = (bf16[256,512]{1,0:T(8,128)(2,1)S(1)}, bf16[256,512]{1,0:T(8,128)(2,1)S(1)}, u32[]{:S(2)}, u32[]{:S(2)}) collective-permute-start(bf16[256,512]{1,0:T(8,128)(2,1)S(1)} %pad_maximum_fusion.8), channel_id=1, source_target_pairs={{0,1},{1,0},{2,3},{3,2},{4,5},{5,4},{6,7},{7,6},{8,9},{9,8},{10,11... | collective-permute-start | bytes 786440 | tf_op jit(solution)/shard_map/ppermute | solution.py:315
  88.2 11.2 %collective-permute-start.12 = (bf16[256,512]{1,0:T(8,128)(2,1)S(1)}, bf16[256,512]{1,0:T(8,128)(2,1)S(1)}, u32[]{:S(2)}, u32[]{:S(2)}) collective-permute-start(bf16[256,512]{1,0:T(8,128)(2,1)S(1)} %pad_maximum_fusion.9), channel_id=1, source_target_pairs={{0,1},{1,0},{2,3},{3,2},{4,5},{5,4},{6,7},{7,6},{8,9},{9,8},{10,11... | collective-permute-start | bytes 786440 | tf_op jit(solution)/shard_map/ppermute | solution.py:315
  89.9 10.8 %collective-permute-start.28 = (bf16[32,8192]{1,0:T(8,128)(2,1)S(1)}, bf16[32,8192]{1,0:T(8,128)(2,1)S(1)}, u32[]{:S(2)}, u32[]{:S(2)}) collective-permute-start(bf16[32,8192]{1,0:T(8,128)(2,1)S(1)} %fusion.3), channel_id=1, source_target_pairs={{4,2},{5,3},{12,10},{13,11},{20,18},{21,19},{28,26},{29,27}} | collective-permute-start | bytes 1572872 | tf_op jit(solution)/shard_map/ppermute | solution.py:315
  93.8 15.8 %collective-permute-start.9 = (bf16[256,1024]{1,0:T(8,128)(2,1)S(1)}, bf16[256,1024]{1,0:T(8,128)(2,1)S(1)}, u32[]{:S(2)}, u32[]{:S(2)}) collective-permute-start(bf16[256,1024]{1,0:T(8,128)(2,1)S(1)} %pad_maximum_fusion.5), channel_id=1, source_target_pairs={{0,1},{1,0},{2,3},{3,2},{4,5},{5,4},{6,7},{7,6},{8,9},{9,8},{10,11... | collective-permute-start | bytes 1572872 | tf_op jit(solution)/shard_map/ppermute | solution.py:315
  99.4 68.2 %collective-permute-start.17 = (bf16[32,8192]{1,0:T(8,128)(2,1)}, bf16[32,8192]{1,0:T(8,128)(2,1)S(1)}, u32[]{:S(2)}, u32[]{:S(2)}) collective-permute-start(bf16[32,8192]{1,0:T(8,128)(2,1)} %add_convert_fusion.3), channel_id=1, source_target_pairs={{2,0},{3,1},{10,8},{11,9},{18,16},{19,17},{26,24},{27,25}} | collective-permute-start | bytes 1572872 | tf_op jit(solution)/shard_map/ppermute | solution.py:315
  100.7 78.2 %collective-permute-start.21 = (bf16[32,8192]{1,0:T(8,128)(2,1)}, bf16[32,8192]{1,0:T(8,128)(2,1)S(1)}, u32[]{:S(2)}, u32[]{:S(2)}) collective-permute-start(bf16[32,8192]{1,0:T(8,128)(2,1)} %add_convert_fusion.2), channel_id=1, source_target_pairs={{2,0},{3,1},{10,8},{11,9},{18,16},{19,17},{26,24},{27,25}} | collective-permute-start | bytes 1572872 | tf_op jit(solution)/shard_map/ppermute | solution.py:315
  109.6 80.5 %collective-permute-start.25 = (bf16[32,8192]{1,0:T(8,128)(2,1)}, bf16[32,8192]{1,0:T(8,128)(2,1)S(1)}, u32[]{:S(2)}, u32[]{:S(2)}) collective-permute-start(bf16[32,8192]{1,0:T(8,128)(2,1)} %add_convert_fusion.1), channel_id=1, source_target_pairs={{2,0},{3,1},{10,8},{11,9},{18,16},{19,17},{26,24},{27,25}} | collective-permute-start | bytes 1572872 | tf_op jit(solution)/shard_map/ppermute | solution.py:315
  110.9 88.8 %collective-permute-start.29 = (bf16[32,8192]{1,0:T(8,128)(2,1)}, bf16[32,8192]{1,0:T(8,128)(2,1)S(1)}, u32[]{:S(2)}, u32[]{:S(2)}) collective-permute-start(bf16[32,8192]{1,0:T(8,128)(2,1)} %add_convert_fusion), channel_id=1, source_target_pairs={{2,0},{3,1},{10,8},{11,9},{18,16},{19,17},{26,24},{27,25}} | collective-permute-start | bytes 1572872 | tf_op jit(solution)/shard_map/ppermute | solution.py:315
  167.7 39.3 %collective-permute-start.13 = (bf16[512,1024]{1,0:T(8,128)(2,1)}, bf16[512,1024]{1,0:T(8,128)(2,1)}, u32[]{:S(2)}, u32[]{:S(2)}) collective-permute-start(bf16[512,1024]{1,0:T(8,128)(2,1)} %shard_map.150), channel_id=1, source_target_pairs={{0,16},{8,24},{16,0},{24,8},{1,17},{9,25},{17,1},{25,9},{2,18},{10... | collective-permute-start | bytes 3145736 | tf_op jit(solution)/shard_map/ppermute | solution.py:315
  178.9 37.6 %collective-permute-start.11 = (bf16[512,1024]{1,0:T(8,128)(2,1)}, bf16[512,1024]{1,0:T(8,128)(2,1)}, u32[]{:S(2)}, u32[]{:S(2)}) collective-permute-start(bf16[512,1024]{1,0:T(8,128)(2,1)} %shard_map.149), channel_id=1, source_target_pairs={{0,16},{8,24},{16,0},{24,8},{1,17},{9,25},{17,1},{25,9},{2,18},{10... | collective-permute-start | bytes 3145736 | tf_op jit(solution)/shard_map/ppermute | solution.py:315
  190.1 48.8 %collective-permute-start.8 = (bf16[512,1024]{1,0:T(8,128)(2,1)}, bf16[512,1024]{1,0:T(8,128)(2,1)}, u32[]{:S(2)}, u32[]{:S(2)}) collective-permute-start(bf16[512,1024]{1,0:T(8,128)(2,1)} %shard_map.148), channel_id=1, source_target_pairs={{0,16},{8,24},{16,0},{24,8},{1,17},{9,25},{17,1},{25,9},{2,18},{10... | collective-permute-start | bytes 3145736 | tf_op jit(solution)/shard_map/ppermute | solution.py:315
  199.7 57.5 %collective-permute-start.6 = (bf16[512,1024]{1,0:T(8,128)(2,1)}, bf16[512,1024]{1,0:T(8,128)(2,1)S(1)}, u32[]{:S(2)}, u32[]{:S(2)}) collective-permute-start(bf16[512,1024]{1,0:T(8,128)(2,1)} %shard_map.147), channel_id=1, source_target_pairs={{0,16},{8,24},{16,0},{24,8},{1,17},{9,25},{17,1},{25,9},{2,18},{10... | collective-permute-start | bytes 3145736 | tf_op jit(solution)/shard_map/ppermute | solution.py:315
  201.3 20.5 %collective-permute-start.1 = (bf16[256,1024]{1,0:T(8,128)(2,1)S(1)}, bf16[256,1024]{1,0:T(8,128)(2,1)S(1)}, u32[]{:S(2)}, u32[]{:S(2)}) collective-permute-start(bf16[256,1024]{1,0:T(8,128)(2,1)S(1)} %pad_maximum_fusion.3), channel_id=1, source_target_pairs={{0,1},{1,0},{2,3},{3,2},{4,5},{5,4},{6,7},{7,6},{8,9},{9,8},{10,11... | collective-permute-start | bytes 1572872 | tf_op jit(solution)/shard_map/ppermute | solution.py:315
  (20 other events, 133.7 us)
